TPU v7x, 512 devices: a whole 4x8x8 slice. The times are simulated.
512 devices in a mesh: fsdp: 16 (over y, x_lo), ed: 32 (over x_hi, z, core).
Axes of the slice: x: 4 (x_hi: 2, x_lo: 2; x = x_hi * 2 + x_lo), y: 8, z: 8, core: 2. Of those that a mesh axis runs over, the one named last changes fastest.
Arguments:
- tokens: bfloat16 [9216, 6144], P('ed', 'fsdp'), may hold values from -6 to 6
- expert_ids: int32 [9216, 2], P('ed'), may hold values from 0 to 7, all different within a row; in each aligned block of 288 rows (0 to 287, 288 to 575, ...) at most 81 rows name the same one
- route_weights: float32 [9216, 2], P('ed'), may hold values from 0.1 to 1
- w_gate: bfloat16 [1, 6144, 8192], P(None, 'fsdp', 'ed'), may hold values from -0.078125 to 0.078125
- w_up: bfloat16 [1, 6144, 8192], P(None, 'fsdp', 'ed'), may hold values from -0.078125 to 0.078125
- w_down: bfloat16 [1, 8192, 6144], P(None, 'ed', 'fsdp'), may hold values from -0.0625 to 0.0625
Outputs:
- mixed: bfloat16 [9216, 6144], P('ed', 'fsdp')
Inputs may be any that keep to these rules, and one draw needn't show every extreme that they name: `expert_ids`: each row names two different experts. In each block of 288 rows that one index of ed holds, no expert is named by more than 81 rows, a bound that some block reaches.
All inputs are finite; a program needn't handle non-finite values.
Results may differ from a plain program's by a relative error of at most 0.025.
Values may be sent and summed in bfloat16 or wider, within the bound.
A program may use at most 64 MiB of HBM per device.

v0:
```python
import jax
import jax.numpy as jnp
from jax import lax
from jax.sharding import PartitionSpec as P

CAP = 81


def slot_match(routes, window, capacity):
    window_ids = jnp.arange(window, dtype=jnp.int32)
    routed = jnp.any(routes[:, :, None, :] == window_ids[None, None, :, None], axis=3)
    position = jnp.cumsum(routed.astype(jnp.int32), axis=1) - 1
    slot_ids = jnp.arange(capacity, dtype=jnp.int32)
    hits = routed[:, :, :, None] & (position[:, :, :, None] == slot_ids[None, None, None, :])
    return hits.astype(jnp.int32)


def take_block(block_rows, row_list):
    return jnp.take(block_rows, row_list, axis=0)


def pick_rows(blocks, routes, window, capacity):
    match = slot_match(routes, window, capacity)
    row_numbers = jnp.arange(blocks.shape[1], dtype=jnp.int32)
    source_row = jnp.sum(match * row_numbers[None, :, None, None], axis=1).reshape(
        blocks.shape[0], window * capacity
    )
    filled = jnp.sum(match, axis=1).reshape(blocks.shape[0], window * capacity)
    picked = jax.vmap(take_block)(blocks, source_row)
    picked = jnp.where(filled[:, :, None] > 0, picked, jnp.zeros_like(picked))
    return picked.reshape(blocks.shape[0], window, capacity, blocks.shape[2])


def combine_matrix(routes, weights, window, capacity):
    match = slot_match(routes[None], window, capacity)[0]
    window_ids = jnp.arange(window, dtype=jnp.int32)
    per_expert = jnp.sum(
        jnp.where(
            routes[:, None, :] == window_ids[None, :, None],
            weights[:, None, :],
            jnp.zeros_like(weights[:, None, :]),
        ),
        axis=2,
    )
    return (per_expert[:, :, None] * match.astype(weights.dtype)).reshape(
        routes.shape[0], window * capacity
    )


def local(tokens, expert_ids, route_weights, w_gate, w_up, w_down):
    window = w_gate.shape[0]
    features_dev = tokens.shape[1]
    hidden_dev = w_gate.shape[2]
    n_ed = lax.axis_size("ed")
    own_slots = pick_rows(tokens[None], expert_ids[None], window, CAP)[0, 0]
    selected = lax.all_gather(own_slots, "ed", axis=0, tiled=True)
    both = jnp.concatenate([w_gate[0], w_up[0]], axis=1)
    partial = jnp.dot(selected, both, preferred_element_type=jnp.float32)
    n_fsdp = lax.axis_size("fsdp")
    rows = partial.shape[0]
    band = -(-rows // (8 * n_fsdp)) * 8
    partial = jnp.pad(partial, ((0, band * n_fsdp - rows), (0, 0)))
    summed = lax.psum_scatter(partial, "fsdp", scatter_dimension=0, tiled=True)
    gate_part = summed[:, :hidden_dev]
    up_part = summed[:, hidden_dev:]
    activation = (jax.nn.silu(gate_part) * up_part).astype(jnp.bfloat16)
    act_rows = lax.all_gather(activation, "fsdp", axis=0, tiled=True)[:rows]
    term = jnp.dot(act_rows, w_down[0], preferred_element_type=jnp.float32)
    term = term.astype(jnp.bfloat16).reshape(n_ed, CAP, features_dev)
    arrived = lax.all_to_all(term, "ed", split_axis=0, concat_axis=0, tiled=True)
    slot_out = jnp.sum(arrived.astype(jnp.float32), axis=0)
    weights_matrix = combine_matrix(expert_ids, route_weights, window, CAP)
    mixed = jnp.dot(
        weights_matrix,
        slot_out.reshape(window * CAP, features_dev),
        precision=lax.Precision.HIGHEST,
        preferred_element_type=jnp.float32,
    )
    return mixed.astype(jnp.bfloat16)


def solution(mesh):
    return jax.shard_map(
        local,
        mesh=mesh,
        in_specs=(
            P("ed", "fsdp"),
            P("ed", None),
            P("ed", None),
            P(None, "fsdp", "ed"),
            P(None, "fsdp", "ed"),
            P(None, "ed", "fsdp"),
        ),
        out_specs=P("ed", "fsdp"),
        check_vma=False,
    )
```

profile of v0, /device:TPU:64, one launch (start us, length us, event | category | flops | bytes accessed | tf_op | source)
XLA Modules:
  0.0 386.1 jit_solution(4538146092871331298)
XLA Ops:
  6.5 0.0 copy-start
  6.5 0.0 all-gather.6.cloned.1.call-start
  6.5 0.7 fusion.18
  7.3 0.3 reduce-window.6
  7.6 0.2 slice_reduce_fusion
  7.8 0.2 reduce-window.9
  8.0 0.1 broadcast.184
  8.1 3.0 convert_reduce_fusion.1
  11.1 0.0 copy-done
  11.1 1.3 gather_fusion
  12.4 0.7 select_bitcast_fusion
  13.2 0.0 all-gather.6.cloned.1.call-update
  13.2 0.0 copy-start.1
  13.2 0.0 copy-start.2
  13.2 0.0 reduce-scatter.2.cloned.1.call-start
  13.3 89.2 %all-gather.6.cloned.1.call-done = bf16[32,81,384]{2,1,0:T(8,128)(2,1)} async-done(((bf16[1,81,384]{2,1,0:T(8,128)(2,1)}), bf16[32,81,384]{2,1,0:T(8,128)(2,1)}) %all-gather.6.cloned.1.call-update) | async-done | bytes 1990672 | tf_op jit(solution)/shard_map/all_gather | solution.py:56
  102.5 1.9 reshape.322
  104.4 0.0 copy-done.1
  104.4 0.0 copy-done.2
  104.4 1.5 fusion.1
  106.0 3.0 pad.9
  108.9 0.0 copy-start.3
  108.9 0.0 reduce-scatter.2.cloned.1.call-update
  109.0 0.0 all-gather.4.cloned.1.call-start
  109.0 125.5 %reduce-scatter.2.cloned.1.call-done = f32[168,512]{1,0:T(8,128)} async-done(((f32[2688,512]{1,0:T(8,128)}), f32[168,512]{1,0:T(8,128)}) %reduce-scatter.2.cloned.1.call-update) | async-done | bytes 344080 | tf_op jit(solution)/shard_map/reduce_scatter | solution.py:63
  234.5 1.7 fusion.6
  236.2 0.0 all-gather.4.cloned.1.call-update
  236.2 73.1 %all-gather.4.cloned.1.call-done = bf16[2688,256]{1,0:T(8,128)(2,1)} async-done(((bf16[168,256]{1,0:T(8,128)(2,1)}), bf16[2688,256]{1,0:T(8,128)(2,1)}) %all-gather.4.cloned.1.call-update) | async-done | bytes 1376272 | tf_op jit(solution)/shard_map/all_gather | solution.py:67
  309.3 0.0 copy-done.3
  309.3 2.2 convolution_convert_fusion
  311.5 1.7 reshape.310
  313.1 0.0 copy-start.4
  313.1 0.0 copy-start.5
  313.2 10.5 %all-to-all-start = ((bf16[32,81,384]{2,1,0:T(8,128)(2,1)}), bf16[32,81,384]{2,1,0:T(8,128)(2,1)S(1)}, u32[]{:S(2)}, u32[]{:S(2)}) async-start(bf16[32,81,384]{2,1,0:T(8,128)(2,1)} %reshape.310), calls=%async_computation.1 | async-start | bytes 4325376 | tf_op jit(solution)/shard_map/all_to_all | solution.py:70
  323.6 0.0 copy-done.4
  323.6 0.0 copy-done.5
  323.7 54.3 %all-to-all-done = bf16[32,81,384]{2,1,0:T(8,128)(2,1)S(1)} async-done(((bf16[32,81,384]{2,1,0:T(8,128)(2,1)}), bf16[32,81,384]{2,1,0:T(8,128)(2,1)S(1)}, u32[]{:S(2)}, u32[]{:S(2)}) %all-to-all-start) | async-done | bytes 1990688 | tf_op jit(solution)/shard_map/all_to_all | solution.py:70
  378.0 0.3 convert_reduce_fusion
  378.3 1.3 convolution_convert_fusion.1
  (11 shorter events, 0.1 us)
Async XLA Ops:
  6.5 4.6 %copy-start = (bf16[288,384]{1,0:T(8,128)(2,1)S(1)}, bf16[288,384]{1,0:T(8,128)(2,1)}, u32[]{:S(2)}) copy-start(bf16[288,384]{1,0:T(8,128)(2,1)} %param.6) | copy-start | bytes 663556
  6.5 96.0 %all-gather.6.cloned.1.call-start = ((), (), s32[]{:S(2)}) async-start(), calls=%async_computation.4 | async-start | bytes 2230272 | tf_op jit(solution)/shard_map/all_gather | solution.py:56
  13.2 91.2 %copy-start.1 = (bf16[1,384,256]{2,1,0:T(8,128)(2,1)S(1)}, bf16[1,384,256]{2,1,0:T(8,128)(2,1)}, u32[]{:S(2)}) copy-start(bf16[1,384,256]{2,1,0:T(8,128)(2,1)} %param.10) | copy-start | bytes 589828
  13.2 91.2 %copy-start.2 = (bf16[1,384,256]{2,1,0:T(8,128)(2,1)S(1)}, bf16[1,384,256]{2,1,0:T(8,128)(2,1)}, u32[]{:S(2)}) copy-start(bf16[1,384,256]{2,1,0:T(8,128)(2,1)} %param.9) | copy-start | bytes 589828
  13.2 221.3 %reduce-scatter.2.cloned.1.call-start = ((), (), s32[]{:S(2)}) async-start(), calls=%async_computation.2 | async-start | bytes 5849088 | tf_op jit(solution)/shard_map/reduce_scatter | solution.py:63
  108.9 200.3 %copy-start.3 = (bf16[1,256,384]{2,1,0:T(8,128)(2,1)S(1)}, bf16[1,256,384]{2,1,0:T(8,128)(2,1)}, u32[]{:S(2)}) copy-start(bf16[1,256,384]{2,1,0:T(8,128)(2,1)} %param.11) | copy-start | bytes 589828
  109.0 200.3 %all-gather.4.cloned.1.call-start = ((), (), s32[]{:S(2)}) async-start(), calls=%async_computation.3 | async-start | bytes 1462272 | tf_op jit(solution)/shard_map/all_gather | solution.py:67
  313.1 10.5 %copy-start.4 = (s32[288,2]{0,1:T(2,128)S(1)}, s32[288,2]{0,1:T(2,128)}, u32[]{:S(2)}) copy-start(s32[288,2]{0,1:T(2,128)} %param.7) | copy-start | bytes 6916
  313.1 10.5 %copy-start.5 = (f32[288,2]{0,1:T(2,128)S(1)}, f32[288,2]{0,1:T(2,128)}, u32[]{:S(2)}) copy-start(f32[288,2]{0,1:T(2,128)} %param.8) | copy-start | bytes 6916
  313.2 64.8 %all-to-all-start = ((bf16[32,81,384]{2,1,0:T(8,128)(2,1)}), bf16[32,81,384]{2,1,0:T(8,128)(2,1)S(1)}, u32[]{:S(2)}, u32[]{:S(2)}) async-start(bf16[32,81,384]{2,1,0:T(8,128)(2,1)} %reshape.310), calls=%async_computation.1 | async-start | bytes 4325376 | tf_op jit(solution)/shard_map/all_to_all | solution.py:70
Sparse Core Ops, SparseCore 0:
  13.3 89.1 all-gather.5
  109.1 125.3 reduce-scatter.1
  236.8 72.4 all-gather.3
where the time goes:
time: 386 us
  waiting for transfers between devices  342 us (89%)
  between operations  13.2 us (3%)
  starting transfers between devices  10.5 us (3%)
  local copies, waits for them, and re-layouts  8.17 us (2%)
  other arithmetic  7.01 us (2%)
  matrix products  5.01 us (1%)
    reduce_scatter x1, waiting for transfers between devices, local(): summed = lax.psum_scatter(partial, 'fsdp', scatter_dimension=0, tiled=True)  125 us
    all_gather x1, waiting for transfers between devices, local(): selected = lax.all_gather(own_slots, 'ed', axis=0, tiled=True)  89.2 us
    all_gather x1, waiting for transfers between devices, local(): act_rows = lax.all_gather(activation, 'fsdp', axis=0, tiled=True)[:rows]  73.1 us
    all_to_all x1, waiting for transfers between devices, local(): lax.all_to_all(term, 'ed', split_axis=0, concat_axis=0, tiled=True)  54.3 us
    all_to_all x1, starting transfers between devices, local(): lax.all_to_all(term, 'ed', split_axis=0, concat_axis=0, tiled=True)  10.5 us
  transfers between devices with their start and end apart: 4, of which 4 were waited for; matrix products, arithmetic and copies ran while one was open for 0% of the time, Pallas kernels for 0%

commit v1 on v0

--- a/solution.py
+++ b/solution.py
@@ -53,7 +53,9 @@
     hidden_dev = w_gate.shape[2]
     n_ed = lax.axis_size("ed")
     own_slots = pick_rows(tokens[None], expert_ids[None], window, CAP)[0, 0]
-    selected = lax.all_gather(own_slots, "ed", axis=0, tiled=True)
+    selected = jnp.concatenate(
+        lax.all_to_all(jnp.stack([own_slots] * lax.axis_size("ed")), "ed", 0, 0), axis=0
+    )
     both = jnp.concatenate([w_gate[0], w_up[0]], axis=1)
     partial = jnp.dot(selected, both, preferred_element_type=jnp.float32)
     n_fsdp = lax.axis_size("fsdp")

time: 386 us -> 362 us (0.938)
  waiting for transfers between devices: 342 us -> 251 us
  blocking collectives: 0 us -> 66.9 us
    all_gather x1 -> x0, waiting for transfers between devices: 89.2 us -> none  [local(): selected = lax.all_gather(own_slots, 'ed', axis=0, tiled=True)]
    all_to_all x0 -> x1, blocking collectives: none -> 66.9 us  [local(): lax.all_to_all(jnp.stack([own_slots] * lax.axis_size('ed')), 'ed', 0, 0)]
  transfers between devices with their start and end apart: 4 -> 3, of which waited for: 4 -> 3; matrix products, arithmetic and copies ran while one was open for 0% -> 0% of each run, Pallas kernels for 0% -> 0%
where the time goes in v1:
time: 362 us; the launch traced here: 361 us
  waiting for transfers between devices  251 us (69%)
  blocking collectives  66.9 us (18%)
  between operations  13.5 us (4%)
  starting transfers between devices  10.5 us (3%)
  local copies, waits for them, and re-layouts  8.41 us (2%)
  other arithmetic  6.38 us (2%)
  matrix products  5.01 us (1%)
    reduce_scatter x1, waiting for transfers between devices, local(): summed = lax.psum_scatter(partial, 'fsdp', scatter_dimension=0, tiled=True)  123 us
    all_gather x1, waiting for transfers between devices, local(): act_rows = lax.all_gather(activation, 'fsdp', axis=0, tiled=True)[:rows]  73.1 us
    all_to_all x1, blocking collectives, local(): lax.all_to_all(jnp.stack([own_slots] * lax.axis_size('ed')), 'ed', 0, 0)  66.9 us
    all_to_all x1, waiting for transfers between devices, local(): lax.all_to_all(term, 'ed', split_axis=0, concat_axis=0, tiled=True)  54.3 us
    all_to_all x1, starting transfers between devices, local(): lax.all_to_all(term, 'ed', split_axis=0, concat_axis=0, tiled=True)  10.5 us
  transfers between devices with their start and end apart: 3, of which 3 were waited for; matrix products, arithmetic and copies ran while one was open for 0% of the time, Pallas kernels for 0%

profile of v1, /device:TPU:64, one launch (start us, length us, event | category | flops | bytes accessed | tf_op | source)
XLA Modules:
  0.0 361.2 jit_solution(5139383004858369607)
XLA Ops:
  6.5 0.0 copy-start
  6.5 0.0 reduce-scatter.2.cloned.1.call-start
  6.5 0.7 fusion.18
  7.3 0.3 reduce-window.6
  7.6 0.2 slice_reduce_fusion
  7.8 0.2 reduce-window.9
  8.0 0.1 broadcast.185
  8.1 3.0 convert_reduce_fusion.1
  11.1 0.0 copy-done
  11.1 1.3 gather_fusion
  12.4 0.1 select_select_fusion
  12.5 0.2 stack.3
  12.7 66.9 %all_to_all.10 = bf16[32,81,384]{2,1,0:T(8,128)(2,1)} all-to-all(bf16[32,81,384]{2,1,0:T(8,128)(2,1)S(1)} %stack.3), channel_id=1, replica_groups=mesh['fsdp'=16,'ed'=32] {'ed'}, dimensions={0} | all-to-all | bytes 3981312 | tf_op jit(solution)/shard_map/all_to_all | solution.py:57
  79.6 0.0 copy-start.1
  79.6 0.0 copy-start.2
  79.6 1.9 reshape.314
  81.5 0.0 copy-done.1
  81.6 0.0 copy-done.2
  81.6 1.5 fusion.1
  83.1 3.0 pad.9
  86.1 0.0 copy-start.3
  86.1 0.0 reduce-scatter.2.cloned.1.call-update
  86.1 0.0 all-gather.2.cloned.1.call-start
  86.2 123.1 %reduce-scatter.2.cloned.1.call-done = f32[168,512]{1,0:T(8,128)} async-done(((f32[2688,512]{1,0:T(8,128)}), f32[168,512]{1,0:T(8,128)}) %reduce-scatter.2.cloned.1.call-update) | async-done | bytes 344080 | tf_op jit(solution)/shard_map/reduce_scatter | solution.py:65
  209.2 1.7 fusion.6
  210.9 0.0 all-gather.2.cloned.1.call-update
  211.0 73.1 %all-gather.2.cloned.1.call-done = bf16[2688,256]{1,0:T(8,128)(2,1)} async-done(((bf16[168,256]{1,0:T(8,128)(2,1)}), bf16[2688,256]{1,0:T(8,128)(2,1)}) %all-gather.2.cloned.1.call-update) | async-done | bytes 1376272 | tf_op jit(solution)/shard_map/all_gather | solution.py:69
  284.0 0.0 copy-done.3
  284.0 2.2 convolution_convert_fusion
  286.2 1.7 reshape.315
  287.9 0.0 copy-start.4
  287.9 0.0 copy-start.5
  287.9 10.5 %all-to-all-start.1 = ((bf16[32,81,384]{2,1,0:T(8,128)(2,1)}), bf16[32,81,384]{2,1,0:T(8,128)(2,1)S(1)}, u32[]{:S(2)}, u32[]{:S(2)}) async-start(bf16[32,81,384]{2,1,0:T(8,128)(2,1)} %reshape.315), calls=%async_computation.2 | async-start | bytes 4325376 | tf_op jit(solution)/shard_map/all_to_all | solution.py:72
  298.4 0.0 copy-done.4
  298.4 0.0 copy-done.5
  298.4 54.3 %all-to-all-done.1 = bf16[32,81,384]{2,1,0:T(8,128)(2,1)S(1)} async-done(((bf16[32,81,384]{2,1,0:T(8,128)(2,1)}), bf16[32,81,384]{2,1,0:T(8,128)(2,1)S(1)}, u32[]{:S(2)}, u32[]{:S(2)}) %all-to-all-start.1) | async-done | bytes 1990688 | tf_op jit(solution)/shard_map/all_to_all | solution.py:72
  352.7 0.3 convert_reduce_fusion
  353.0 1.3 convolution_convert_fusion.1
  (11 shorter events, 0.1 us)
Async XLA Ops:
  6.5 4.6 %copy-start = (bf16[288,384]{1,0:T(8,128)(2,1)S(1)}, bf16[288,384]{1,0:T(8,128)(2,1)}, u32[]{:S(2)}) copy-start(bf16[288,384]{1,0:T(8,128)(2,1)} %param.6) | copy-start | bytes 663556
  6.5 202.7 %reduce-scatter.2.cloned.1.call-start = ((), (), s32[]{:S(2)}) async-start(), calls=%async_computation.3 | async-start | bytes 5849088 | tf_op jit(solution)/shard_map/reduce_scatter | solution.py:65
  79.6 1.9 copy-start.1
  79.6 2.0 copy-start.2
  86.1 197.9 %copy-start.3 = (bf16[1,256,384]{2,1,0:T(8,128)(2,1)S(1)}, bf16[1,256,384]{2,1,0:T(8,128)(2,1)}, u32[]{:S(2)}) copy-start(bf16[1,256,384]{2,1,0:T(8,128)(2,1)} %param.11) | copy-start | bytes 589828
  86.1 197.9 %all-gather.2.cloned.1.call-start = ((), (), s32[]{:S(2)}) async-start(), calls=%async_computation.4 | async-start | bytes 1462272 | tf_op jit(solution)/shard_map/all_gather | solution.py:69
  287.9 10.5 %copy-start.4 = (s32[288,2]{0,1:T(2,128)S(1)}, s32[288,2]{0,1:T(2,128)}, u32[]{:S(2)}) copy-start(s32[288,2]{0,1:T(2,128)} %param.7) | copy-start | bytes 6916
  287.9 10.5 %copy-start.5 = (f32[288,2]{0,1:T(2,128)S(1)}, f32[288,2]{0,1:T(2,128)}, u32[]{:S(2)}) copy-start(f32[288,2]{0,1:T(2,128)} %param.8) | copy-start | bytes 6916
  287.9 64.8 %all-to-all-start.1 = ((bf16[32,81,384]{2,1,0:T(8,128)(2,1)}), bf16[32,81,384]{2,1,0:T(8,128)(2,1)S(1)}, u32[]{:S(2)}, u32[]{:S(2)}) async-start(bf16[32,81,384]{2,1,0:T(8,128)(2,1)} %reshape.315), calls=%async_computation.2 | async-start | bytes 4325376 | tf_op jit(solution)/shard_map/all_to_all | solution.py:72
Sparse Core Ops, SparseCore 0:
  86.2 122.9 reduce-scatter.1
  211.5 72.4 all-gather.1
